TPU v7x, 128 devices: a whole 4x4x4 slice. The times are simulated.
128 devices in a mesh: dp: 4 (over y), expert: 32 (over x, z, core).
Axes of the slice: x: 4, y: 4, z: 4, core: 2. Of those that a mesh axis runs over, the one named last changes fastest.
Arguments:
- hidden_in: bfloat16 [32768, 1024], P(('dp', 'expert')), may hold values from -6 to 6
- moe_gain: float32 [1024], replicated, may hold values from 0.1 to 1.9
- router_weight: bfloat16 [1024, 64], replicated, may hold values from -0.1875 to 0.1875
- expert_gate: bfloat16 [64, 1024, 1024], P('expert'), may hold values from -0.1875 to 0.1875
- expert_up: bfloat16 [64, 1024, 1024], P('expert'), may hold values from -0.1875 to 0.1875
- expert_down: bfloat16 [64, 1024, 1024], P('expert'), may hold values from -0.1875 to 0.1875
- final_gain: float32 [1024], replicated, may hold values from 0.1 to 1.9
- vocab_weight: bfloat16 [1024, 32768], P(None, 'expert'), may hold values from -24 to 24
- token_ids: int32 [32768], P(('dp', 'expert')), may hold values from 0 to 32767
- doc_ids: int32 [32768], P(('dp', 'expert')), may hold values from 0 to 511, as said below
- routes: int32 [32768, 2], P(('dp', 'expert')), may hold values from 0 to 63, all different within a row; in each aligned block of 256 rows (0 to 255, 256 to 511, ...) at most 16 rows name the same one
Outputs:
- token_loss: float32 [32768], P(('dp', 'expert'))
- doc_score: float32 [512], P(('dp', 'expert'))
Inputs may be any that keep to these rules, and one draw needn't show every extreme that they name: `routes`: among the rows of one device no expert is named more than 16 times; in every draw some expert is named exactly 16 times by the rows of some device. `doc_ids`: documents are numbered in the order of the stream; each document is one run of consecutive tokens, shorter than 512; every document number is used; the rows of each device hold the first tokens of exactly 4 documents.
All inputs are finite; a program needn't handle non-finite values.
Results may differ from a plain program's by a relative error of at most 0.0031.
Values may be sent and summed in bfloat16 or wider, within the bound.
A program may use at most 128 MiB of HBM per device.

v0:
```python
import jax
import jax.numpy as jnp
from jax import lax
from jax.sharding import Mesh
from jax.sharding import PartitionSpec as P

TOP = 2
DOC_DEV = 4
EXPERT = ("expert_0", "expert_1", "expert_2")
DP_EXPERT = ("dp", "expert_0", "expert_1", "expert_2")
EPSILON = 1e-06


def shifted(value, axis, steps):
    count = lax.axis_size(axis)
    first, last = (max(0, -steps), min(count, count - steps))
    return lax.ppermute(value, axis, [(source, source + steps) for source in range(first, last)])


def gathered_once(value, axis):
    leaves = jax.tree.leaves(value)
    sequence = sorted(range(len(leaves)), key=lambda k: -leaves[k].size)
    width = (1, *leaves[sequence[0]].shape)[-1]
    lines = [
        jnp.pad(leaves[k].reshape(-1), (0, -leaves[k].size % width)).reshape(-1, width)
        for k in sequence
    ]
    both, at, found = (lax.all_gather(jnp.concatenate(lines), axis), 0, {})
    for k, line in zip(sequence, lines):
        slab = both[:, at : at + len(line)].reshape(len(both), -1)
        found[k] = slab[:, : leaves[k].size].reshape(-1, *leaves[k].shape)
        at += len(line)
    numbers = iter(range(len(leaves)))
    return jax.tree.map(lambda _: found[next(numbers)], value)


def merged_by_axis(value, axes, combine):
    for axis in axes:
        pieces = gathered_once(value, axis)
        value = jax.tree.map(lambda part: part[0], pieces)
        for k in range(1, lax.axis_size(axis)):
            value = combine(value, jax.tree.map(lambda part: part[k], pieces))
    return value


def by_axis(value, axes):
    for axis in axes:
        value = lax.psum(value, axis)
    return value


def normalize(values, gain_vector):
    inv_scale = lax.rsqrt(jnp.mean(values * values, axis=-1, keepdims=True) + EPSILON)
    return values * inv_scale * gain_vector


def stats_block(hidden_rows, wanted, vocab_weight, voc_start):
    scores = jnp.dot(hidden_rows, vocab_weight, preferred_element_type=jnp.float32)
    highest = jnp.max(scores, axis=1)
    totals = jnp.sum(jnp.exp(scores - highest[:, None]), axis=1)
    columns = voc_start + lax.broadcasted_iota(jnp.int32, scores.shape, 1)
    picked = jnp.sum(jnp.where(columns == wanted[:, None], scores, 0.0), axis=1)
    return (highest, totals, picked)


def row_stats(hidden_rows, wanted, vocab_weight, voc_start):
    row_count = hidden_rows.shape[0]

    def one_block(packed):
        return stats_block(packed[0], packed[1], vocab_weight, voc_start)

    blocks = lax.map(
        one_block,
        (
            hidden_rows.reshape(row_count // 1024, 1024, hidden_rows.shape[1]),
            wanted.reshape(row_count // 1024, 1024),
        ),
    )
    return tuple((member.reshape(row_count) for member in blocks))


def join_rows(first, second):
    highest = jnp.maximum(first[0], second[0])
    totals = first[1] * jnp.exp(first[0] - highest) + second[1] * jnp.exp(second[0] - highest)
    return (highest, totals, first[2] + second[2])


def local(
    hidden_in,
    moe_gain,
    router_weight,
    expert_gate,
    expert_up,
    expert_down,
    final_gain,
    vocab_weight,
    token_ids,
    doc_ids,
    routes,
):
    tok_rows, width = hidden_in.shape
    owners = lax.axis_size(EXPERT)
    local_experts = expert_gate.shape[0]
    experts = owners * local_experts
    slot_count = max(2, 2 * TOP * tok_rows // experts)
    residual = hidden_in.astype(jnp.float32)
    normed = normalize(residual, moe_gain).astype(jnp.bfloat16)
    router_scores = jnp.dot(normed, router_weight, preferred_element_type=jnp.float32)
    chosen = routes[:, :, None] == lax.broadcasted_iota(jnp.int32, (tok_rows, TOP, experts), 2)
    picked_scores = jnp.sum(jnp.where(chosen, router_scores[:, None, :], 0.0), axis=2)
    first_gate = jax.nn.sigmoid(picked_scores[:, 0] - picked_scores[:, 1])
    second_gate = 1.0 - first_gate
    flat_routes = routes.reshape(tok_rows * TOP)
    one_hot = (
        flat_routes[:, None] == lax.broadcasted_iota(jnp.int32, (tok_rows * TOP, experts), 1)
    ).astype(jnp.int32)
    slot_index = jnp.sum(one_hot * jnp.cumsum(one_hot, axis=0), axis=1) - 1
    position = flat_routes * slot_count + slot_index
    slot_iota = lax.broadcasted_iota(jnp.int32, (tok_rows * TOP, experts * slot_count), 1)
    placement = (
        (position[:, None] == slot_iota)
        .astype(jnp.bfloat16)
        .reshape(tok_rows, TOP, experts * slot_count)
    )
    first_place = placement[:, 0, :]
    second_place = placement[:, 1, :]
    dispatch_map = first_place + second_place
    outgoing = lax.dot_general(
        dispatch_map, normed, (((0,), (0,)), ((), ())), preferred_element_type=jnp.float32
    )
    outgoing = outgoing.astype(jnp.bfloat16).reshape(owners, local_experts, slot_count, width)
    arrived = lax.all_to_all(outgoing, EXPERT, split_axis=0, concat_axis=0, tiled=True)
    gate_part = jnp.einsum(
        "sekd,edf->sekf", arrived, expert_gate, preferred_element_type=jnp.float32
    )
    up_part = jnp.einsum("sekd,edf->sekf", arrived, expert_up, preferred_element_type=jnp.float32)
    active = (jax.nn.silu(gate_part) * up_part).astype(jnp.bfloat16)
    expert_result = jnp.einsum(
        "sekf,efd->sekd", active, expert_down, preferred_element_type=jnp.float32
    ).astype(jnp.bfloat16)
    returned = lax.all_to_all(
        expert_result, EXPERT, split_axis=0, concat_axis=0, tiled=True
    ).reshape(experts * slot_count, width)
    first_rows = jnp.dot(first_place, returned, preferred_element_type=jnp.float32)
    second_rows = jnp.dot(second_place, returned, preferred_element_type=jnp.float32)
    mixed = residual + (first_gate[:, None] * first_rows + second_gate[:, None] * second_rows)
    final_rows = normalize(mixed, final_gain).astype(jnp.bfloat16)
    following = shifted((token_ids[:1], doc_ids[:1]), DP_EXPERT, -1)
    targets = jnp.concatenate([token_ids[1:], following[0]])
    counted = jnp.concatenate([doc_ids[1:], following[1]]) == doc_ids
    voc_start = lax.axis_index(EXPERT) * vocab_weight.shape[1]
    fresh = row_stats(
        lax.all_gather(final_rows, EXPERT, axis=0, tiled=True),
        lax.all_gather(targets, EXPERT, axis=0, tiled=True),
        vocab_weight,
        voc_start,
    )
    row_highest, row_totals, row_picked = tuple((update for update in fresh))
    own_start = lax.axis_index(EXPERT) * tok_rows
    merged = merged_by_axis((row_highest, row_totals, row_picked), EXPERT, join_rows)
    own_high = lax.dynamic_slice_in_dim(merged[0], own_start, tok_rows, 0)
    own_totals = lax.dynamic_slice_in_dim(merged[1], own_start, tok_rows, 0)
    target_score = lax.dynamic_slice_in_dim(merged[2], own_start, tok_rows, 0)
    log_norm = own_high + jnp.log(own_totals)
    token_loss = jnp.where(counted, log_norm - target_score, 0.0)
    devices = lax.axis_size("dp") * owners
    documents = DOC_DEV * devices
    doc_start = (lax.axis_index("dp") * owners + lax.axis_index(EXPERT)) * DOC_DEV
    member_map = (
        doc_ids[:, None] == lax.broadcasted_iota(jnp.int32, (tok_rows, documents), 1)
    ).astype(jnp.float32)
    partial_loss = jnp.dot(token_loss, member_map, precision=lax.Precision.HIGHEST)
    partial_length = jnp.sum(member_map, axis=0)
    whole_loss, whole_length = (
        by_axis(partial_loss, DP_EXPERT),
        by_axis(partial_length, DP_EXPERT),
    )
    loss_sum = jnp.sum(whole_loss)
    doc_loss = lax.dynamic_slice_in_dim(whole_loss, doc_start, DOC_DEV, 0)
    doc_length = lax.dynamic_slice_in_dim(whole_length, doc_start, DOC_DEV, 0)
    global_mean = loss_sum / (tok_rows * devices - documents)
    doc_score = doc_loss / doc_length - global_mean
    return (token_loss, doc_score)


def solution(mesh):
    split = Mesh(
        mesh.devices.reshape(mesh.shape["dp"], 4, 4, 2), ("dp", "expert_0", "expert_1", "expert_2")
    )
    in_specs = (
        P(DP_EXPERT, None),
        P(),
        P(),
        P(EXPERT, None, None),
        P(EXPERT, None, None),
        P(EXPERT, None, None),
        P(),
        P(None, EXPERT),
        P(DP_EXPERT),
        P(DP_EXPERT),
        P(DP_EXPERT, None),
    )
    out_specs = (P(DP_EXPERT), P(DP_EXPERT))
    return jax.shard_map(local, mesh=split, in_specs=in_specs, out_specs=out_specs, check_vma=False)
```

profile of v0, /device:TPU:1, one launch (start us, length us, event | category | flops | bytes accessed | tf_op | source)
XLA Modules:
  0.0 299.3 jit_solution(4102769667074141839)
XLA Ops:
  12.7 1.9 convolution_convert_fusion
  14.7 37.4 %all_to_all.10 = bf16[32,2,16,1024]{3,2,1,0:T(8,128)(2,1)S(1)} all-to-all(bf16[32,2,16,1024]{3,2,1,0:T(8,128)(2,1)S(1)} %bitcast.274), channel_id=1, replica_groups=mesh['dp'=4,'expert_0'=4,'expert_1'=4,'expert_2'=2] {'expert_0','expert_..., dimensions={0} | all-to-all | bytes 4194304 | tf_op jit(solution)/shard_map/all_to_all | solution.py:132
  52.0 4.3 %fusion.8 = f32[2,32,16,1024]{3,2,1,0:T(8,128)} fusion(bf16[2,1024,1024]{2,1,0:T(8,128)(2,1)S(1)} %copy-done.7, bf16[32,2,16,1024]{3,2,1,0:T(8,128)(2,1)S(1)} %all_to_all.10), kind=kOutput, calls=%fused_computation.12 | convolution fusion | flops 2147483648 | bytes 10485760 | tf_op jit(solution)/shard_map/sekd,edf->sekf/dot_general | solution.py:133
  56.4 10.7 %convert_bitcast_fusion = bf16[32,2,16,1024]{3,2,0,1:T(8,128)(2,1)} fusion(bf16[2,1024,1024]{2,1,0:T(8,128)(2,1)} %param.18, f32[2,32,16,1024]{3,2,1,0:T(8,128)} %fusion.8, bf16[2,1024,1024]{2,1,0:T(8,128)(2,1)} %param.17, bf16[32,2,16,1024]{3,2,1,0:T(8,128)(2,1)S(1)} %all_to_all.10), kind=kOutput, calls=%fused_computation.21 | convolution fusion | flops 4302307328 | bytes 16777216 | tf_op jit(solution)/shard_map/sekf,efd->sekd/dot_general | solution.py:138
  67.0 3.3 %copy.53 = bf16[32,2,16,1024]{3,2,1,0:T(8,128)(2,1)} copy(bf16[32,2,16,1024]{3,2,0,1:T(8,128)(2,1)} %convert_bitcast_fusion) | data formatting | bytes 4194304 | tf_op jit(solution)/shard_map/convert_element_type | solution.py:140
  70.4 3.9 %all-to-all-start.1 = ((bf16[32,2,16,1024]{3,2,1,0:T(8,128)(2,1)}), bf16[32,2,16,1024]{3,2,1,0:T(8,128)(2,1)S(1)}, u32[]{:S(2)}, u32[]{:S(2)}) async-start(bf16[32,2,16,1024]{3,2,1,0:T(8,128)(2,1)} %copy.53), calls=%async_computation.1 | async-start | bytes 4194304 | tf_op jit(solution)/shard_map/all_to_all | solution.py:141
  74.8 27.8 %all-to-all-done.1 = bf16[32,2,16,1024]{3,2,1,0:T(8,128)(2,1)S(1)} async-done(((bf16[32,2,16,1024]{3,2,1,0:T(8,128)(2,1)}), bf16[32,2,16,1024]{3,2,1,0:T(8,128)(2,1)S(1)}, u32[]{:S(2)}, u32[]{:S(2)}) %all-to-all-start.1) | async-done | bytes 2097184 | tf_op jit(solution)/shard_map/all_to_all | solution.py:141
  105.9 2.8 collective-permute-start.1
  109.2 1.9 collective-permute-start
  112.1 24.1 %all-gather.3 = s32[32,1,256]{2,1,0:T(1,128)S(1)} all-gather(s32[1,1,256]{2,1,0:T(1,128)S(1)} %bitcast.293), channel_id=1, replica_groups=mesh['dp'=4,'expert_0'=4,'expert_1'=4,'expert_2'=2] {'expert_0','expert_..., dimensions={0}, use_global_device_ids=true | all-gather | bytes 33792 | tf_op jit(solution)/shard_map/all_gather | solution.py:154
  136.4 39.9 %all-gather.9.cloned.1.call-done = bf16[8192,1024]{1,0:T(8,128)(2,1)} async-done(((bf16[256,1024]{1,0:T(8,128)(2,1)}), bf16[8192,1024]{1,0:T(8,128)(2,1)}) %all-gather.9.cloned.1.call-update) | async-done | bytes 16777232 | tf_op jit(solution)/shard_map/all_gather | solution.py:153
  176.2 52.1 %while.14 = (s32[]{:T(128)}, f32[8,1024]{1,0:T(8,128)S(1)}, f32[8,1024]{1,0:T(8,128)S(1)}, f32[8,1024]{1,0:T(8,128)S(1)}, bf16[8,1024,1024]{2,1,0:T(8,128)(2,1)}...) while((s32[]{:T(128)}, f32[8,1024]{1,0:T(8,128)S(1)}, ...), condition=%wide.region_10.11_spmd, body=%wide.region_6.10_spmd.sunk | while | flops 2153773056 | bytes 12644985 | solution.py:72
  176.2 4.7 %fusion.87 = (f32[1024]{0:T(1024)S(1)}, f32[1024,1024]{0,1:T(8,128)S(1)}) fusion(bf16[1024,1024]{1,0:T(8,128)(2,1)} %get-tuple-element.175, bf16[8,1024,1024]{2,1,0:T(8,128)(2,1)} %get-tuple-element.174, s32[]{:T(128)} %get-tuple-element.160), kind=kOutput, calls=%fused_computation.133.clone.1 | convolution fusion | flops 2148531200 | bytes 8393216 | tf_op jit(solution)/shard_map/while/body/eval_jaxpr/dot_general | solution.py:58
  181.0 1.4 select_reduce_fusion.3
  182.8 4.7 %fusion.87 = (f32[1024]{0:T(1024)S(1)}, f32[1024,1024]{0,1:T(8,128)S(1)}) fusion(bf16[1024,1024]{1,0:T(8,128)(2,1)} %get-tuple-element.175, bf16[8,1024,1024]{2,1,0:T(8,128)(2,1)} %get-tuple-element.174, s32[]{:T(128)} %get-tuple-element.160), kind=kOutput, calls=%fused_computation.133.clone.1 | convolution fusion | flops 2148531200 | bytes 8393216 | tf_op jit(solution)/shard_map/while/body/eval_jaxpr/dot_general | solution.py:58
  187.5 1.4 select_reduce_fusion.3
  189.3 4.7 %fusion.87 = (f32[1024]{0:T(1024)S(1)}, f32[1024,1024]{0,1:T(8,128)S(1)}) fusion(bf16[1024,1024]{1,0:T(8,128)(2,1)} %get-tuple-element.175, bf16[8,1024,1024]{2,1,0:T(8,128)(2,1)} %get-tuple-element.174, s32[]{:T(128)} %get-tuple-element.160), kind=kOutput, calls=%fused_computation.133.clone.1 | convolution fusion | flops 2148531200 | bytes 8393216 | tf_op jit(solution)/shard_map/while/body/eval_jaxpr/dot_general | solution.py:58
  194.0 1.4 select_reduce_fusion.3
  195.8 4.7 %fusion.87 = (f32[1024]{0:T(1024)S(1)}, f32[1024,1024]{0,1:T(8,128)S(1)}) fusion(bf16[1024,1024]{1,0:T(8,128)(2,1)} %get-tuple-element.175, bf16[8,1024,1024]{2,1,0:T(8,128)(2,1)} %get-tuple-element.174, s32[]{:T(128)} %get-tuple-element.160), kind=kOutput, calls=%fused_computation.133.clone.1 | convolution fusion | flops 2148531200 | bytes 8393216 | tf_op jit(solution)/shard_map/while/body/eval_jaxpr/dot_general | solution.py:58
  200.5 1.4 select_reduce_fusion.3
  202.3 4.7 %fusion.87 = (f32[1024]{0:T(1024)S(1)}, f32[1024,1024]{0,1:T(8,128)S(1)}) fusion(bf16[1024,1024]{1,0:T(8,128)(2,1)} %get-tuple-element.175, bf16[8,1024,1024]{2,1,0:T(8,128)(2,1)} %get-tuple-element.174, s32[]{:T(128)} %get-tuple-element.160), kind=kOutput, calls=%fused_computation.133.clone.1 | convolution fusion | flops 2148531200 | bytes 8393216 | tf_op jit(solution)/shard_map/while/body/eval_jaxpr/dot_general | solution.py:58
  207.0 1.4 select_reduce_fusion.3
  208.8 4.7 %fusion.87 = (f32[1024]{0:T(1024)S(1)}, f32[1024,1024]{0,1:T(8,128)S(1)}) fusion(bf16[1024,1024]{1,0:T(8,128)(2,1)} %get-tuple-element.175, bf16[8,1024,1024]{2,1,0:T(8,128)(2,1)} %get-tuple-element.174, s32[]{:T(128)} %get-tuple-element.160), kind=kOutput, calls=%fused_computation.133.clone.1 | convolution fusion | flops 2148531200 | bytes 8393216 | tf_op jit(solution)/shard_map/while/body/eval_jaxpr/dot_general | solution.py:58
  215.3 4.7 %fusion.87 = (f32[1024]{0:T(1024)S(1)}, f32[1024,1024]{0,1:T(8,128)S(1)}) fusion(bf16[1024,1024]{1,0:T(8,128)(2,1)} %get-tuple-element.175, bf16[8,1024,1024]{2,1,0:T(8,128)(2,1)} %get-tuple-element.174, s32[]{:T(128)} %get-tuple-element.160), kind=kOutput, calls=%fused_computation.133.clone.1 | convolution fusion | flops 2148531200 | bytes 8393216 | tf_op jit(solution)/shard_map/while/body/eval_jaxpr/dot_general | solution.py:58
  221.8 4.7 %fusion.87 = (f32[1024]{0:T(1024)S(1)}, f32[1024,1024]{0,1:T(8,128)S(1)}) fusion(bf16[1024,1024]{1,0:T(8,128)(2,1)} %get-tuple-element.175, bf16[8,1024,1024]{2,1,0:T(8,128)(2,1)} %get-tuple-element.174, s32[]{:T(128)} %get-tuple-element.160), kind=kOutput, calls=%fused_computation.133.clone.1 | convolution fusion | flops 2148531200 | bytes 8393216 | tf_op jit(solution)/shard_map/while/body/eval_jaxpr/dot_general | solution.py:58
  228.5 11.0 %all-gather.4 = f32[4,3,8192]{2,1,0:T(4,128)S(1)} all-gather(f32[1,3,8192]{2,1,0:T(4,128)S(1)} %maximum_bitcast_fusion), channel_id=2, replica_groups=mesh['dp'=4,'expert_0'=4,'expert_1'=4,'expert_2'=2] {'expert_0'}, dimensions={0}, use_global_device_ids=true | all-gather | bytes 491520 | tf_op jit(solution)/shard_map/all_gather | solution.py:28
  240.1 9.9 %all-gather.5 = f32[4,3,8192]{2,1,0:T(4,128)S(1)} all-gather(f32[1,3,8192]{2,1,0:T(4,128)S(1)} %maximum_bitcast_fusion.1), channel_id=3, replica_groups=mesh['dp'=4,'expert_0'=4,'expert_1'=4,'expert_2'=2] {'expert_1'}, dimensions={0}, use_global_device_ids=true | all-gather | bytes 491520 | tf_op jit(solution)/shard_map/all_gather | solution.py:28
  250.5 6.9 %all-gather.6 = f32[2,3,8192]{2,1,0:T(4,128)S(1)} all-gather(f32[1,3,8192]{2,1,0:T(4,128)S(1)} %maximum_bitcast_fusion.2), channel_id=4, replica_groups=mesh['dp'=4,'expert_0'=4,'expert_1'=4,'expert_2'=2] {'expert_2'}, dimensions={0}, use_global_device_ids=true | all-gather | bytes 294912 | tf_op jit(solution)/shard_map/all_gather | solution.py:28
  258.7 8.4 %all-reduce.2 = (f32[512]{0:T(512)S(1)}, f32[512]{0:T(512)S(1)}) all-reduce(f32[512]{0:T(512)S(1)} %convert_reduce_fusion, f32[512]{0:T(512)S(1)} %bitcast.294), channel_id=1, replica_groups=mesh['dp'=4,'expert_0'=4,'expert_1'=4,'expert_2'=2] {'dp'}, use_global_device_ids=true, to_apply=%region_16.17 | all-reduce | flops 1024 | bytes 8192 | tf_op jit(solution)/shard_map/psum | solution.py:48
  267.2 8.7 %all-reduce.1 = (f32[512]{0:T(512)S(1)}, f32[512]{0:T(512)S(1)}) all-reduce(f32[512]{0:T(512)S(1)} %get-tuple-element.71, f32[512]{0:T(512)S(1)} %get-tuple-element.72), channel_id=1, replica_groups=mesh['dp'=4,'expert_0'=4,'expert_1'=4,'expert_2'=2] {'expert_0'}, use_global_device_ids=true, to_apply=%region_17.18 | all-reduce | flops 1024 | bytes 8192 | tf_op jit(solution)/shard_map/psum | solution.py:48
  275.8 6.3 %all-reduce = (f32[512]{0:T(512)S(1)}, f32[512]{0:T(512)S(1)}) all-reduce(f32[512]{0:T(512)S(1)} %get-tuple-element.69, f32[512]{0:T(512)S(1)} %get-tuple-element.70), channel_id=1, replica_groups=mesh['dp'=4,'expert_0'=4,'expert_1'=4,'expert_2'=2] {'expert_1'}, use_global_device_ids=true, to_apply=%region_18.19 | all-reduce | flops 1024 | bytes 8192 | tf_op jit(solution)/shard_map/psum | solution.py:48
  282.1 8.5 %all-reduce.3 = (f32[512]{0:T(512)S(1)}, f32[512]{0:T(512)S(1)}) all-reduce(f32[512]{0:T(512)S(1)} %get-tuple-element.67, f32[512]{0:T(512)S(1)} %get-tuple-element.68), channel_id=1, replica_groups=mesh['dp'=4,'expert_0'=4,'expert_1'=4,'expert_2'=2] {'expert_2'}, use_global_device_ids=true, to_apply=%region_19.20 | all-reduce | flops 1024 | bytes 8192 | tf_op jit(solution)/shard_map/psum | solution.py:48
  (116 shorter events, 21.5 us)
Async XLA Ops:
  7.2 67.2 %copy-start = (bf16[1024,64]{0,1:T(8,128)(2,1)S(1)}, bf16[1024,64]{0,1:T(8,128)(2,1)}, u32[]{:S(2)}) copy-start(bf16[1024,64]{0,1:T(8,128)(2,1)} %param.15) | copy-start | bytes 393220
  11.3 40.7 %copy-start.7 = (bf16[2,1024,1024]{2,1,0:T(8,128)(2,1)S(1)}, bf16[2,1024,1024]{2,1,0:T(8,128)(2,1)}, u32[]{:S(2)}) copy-start(bf16[2,1024,1024]{2,1,0:T(8,128)(2,1)} %param.16) | copy-start | bytes 12582916
  67.0 7.3 %copy-start.1 = (bf16[256,1024]{1,0:T(8,128)(2,1)S(1)}, bf16[256,1024]{1,0:T(8,128)(2,1)}, u32[]{:S(2)}) copy-start(bf16[256,1024]{1,0:T(8,128)(2,1)} %param.13) | copy-start | bytes 1572868
  67.0 7.3 %copy-start.8 = (f32[1024]{0:T(1024)S(1)}, f32[1024]{0:T(1024)}, u32[]{:S(2)}) copy-start(f32[1024]{0:T(1024)} %param.14) | copy-start | bytes 12292
  67.0 7.7 %copy-start.2 = (s32[256,2]{0,1:T(2,128)S(1)}, s32[256,2]{0,1:T(2,128)}, u32[]{:S(2)}) copy-start(s32[256,2]{0,1:T(2,128)} %param.23) | copy-start | bytes 6148
  70.4 32.3 %all-to-all-start.1 = ((bf16[32,2,16,1024]{3,2,1,0:T(8,128)(2,1)}), bf16[32,2,16,1024]{3,2,1,0:T(8,128)(2,1)S(1)}, u32[]{:S(2)}, u32[]{:S(2)}) async-start(bf16[32,2,16,1024]{3,2,1,0:T(8,128)(2,1)} %copy.53), calls=%async_computation.1 | async-start | bytes 4194304 | tf_op jit(solution)/shard_map/all_to_all | solution.py:141
  74.3 101.9 %all-gather.9.cloned.1.call-start = ((), (), s32[]{:S(2)}) async-start(), calls=%async_computation.2 | async-start | bytes 17301504 | tf_op jit(solution)/shard_map/all_gather | solution.py:153
  102.6 1.7 copy-start.4
  103.4 2.0 copy-start.6
  103.4 5.3 %copy-start.3 = (s32[256]{0:T(256)S(1)}, s32[256]{0:T(256)}, u32[]{:S(2)}) copy-start(s32[256]{0:T(256)} %param.22) | copy-start | bytes 3076
  105.9 5.5 %collective-permute-start.1 = (s32[1]{0:T(128)}, s32[1]{0:T(128)}, u32[]{:S(2)}, u32[]{:S(2)}) collective-permute-start(s32[1]{0:T(128)} %slice.204), channel_id=1, source_target_pairs={{1,0},{2,1},{3,2},{4,3},{5,4},{6,5},{7,6},{8,7},{9,8},{10,9},{11,1... | collective-permute-start | bytes 20 | tf_op jit(solution)/shard_map/ppermute | solution.py:17
  109.2 148.4 %collective-permute-start = (s32[1]{0:T(128)}, s32[1]{0:T(128)}, u32[]{:S(2)}, u32[]{:S(2)}) collective-permute-start(s32[1]{0:T(128)} %slice.194), channel_id=1, source_target_pairs={{1,0},{2,1},{3,2},{4,3},{5,4},{6,5},{7,6},{8,7},{9,8},{10,9},{11,1... | collective-permute-start | bytes 20 | tf_op jit(solution)/shard_map/ppermute | solution.py:17
  258.4 34.1 %copy-start.5 = (f32[256]{0:T(256)}, f32[256]{0:T(256)S(1)}, u32[]{:S(2)}) copy-start(f32[256]{0:T(256)S(1)} %compare_select_fusion) | copy-start | bytes 3076
Sparse Core Ops, SparseCore 0:
  105.5 70.7 all-gather.8
where the time goes:
time: 300 us; the launch traced here: 299 us
  blocking collectives  121 us (40%)
  waiting for transfers between devices  67.7 us (23%)
  matrix products  56.8 us (19%)
  other arithmetic  20.3 us (7%)
  between operations  15 us (5%)
  local copies, waits for them, and re-layouts  9.12 us (3%)
  starting transfers between devices  8.66 us (3%)
    all_gather x1, waiting for transfers between devices, local(): lax.all_gather(final_rows, EXPERT, axis=0, tiled=True)  39.9 us
    dot_general x8, matrix products, stats_block(): jnp.dot(hidden_rows, vocab_weight, preferred_element_type=jnp.float32)  37.5 us
    all_to_all x1, blocking collectives, local(): lax.all_to_all(outgoing, EXPERT, split_axis=0, concat_axis=0, tiled=True)  37.4 us
    psum x4, blocking collectives, by_axis(): value = lax.psum(value, axis)  31.9 us
    all_to_all x1, waiting for transfers between devices, local(): lax.all_to_all(expert_result, EXPERT, split_axis=0, concat_axis=0, tiled=...  27.8 us
    all_gather x3, blocking collectives, gathered_once(): both, at, found = (lax.all_gather(jnp.concatenate(lines), axis), 0, {})  27.8 us
    all_gather x1, blocking collectives, local(): lax.all_gather(targets, EXPERT, axis=0, tiled=True)  24.1 us
    reduce_sum x8, other arithmetic, stats_block(): picked = jnp.sum(jnp.where(columns == wanted[:, None], scores, 0.0), axis=1)  11.3 us
  transfers between devices with their start and end apart: 4, of which 2 were waited for; matrix products, arithmetic and copies ran while one was open for 19% of the time, Pallas kernels for 0%

commit v1 on v0

--- a/solution.py
+++ b/solution.py
@@ -1,3 +1,4 @@
+import functools
 import jax
 import jax.numpy as jnp
 from jax import lax
@@ -9,6 +10,18 @@
 EXPERT = ("expert_0", "expert_1", "expert_2")
 DP_EXPERT = ("dp", "expert_0", "expert_1", "expert_2")
 EPSILON = 1e-06
+
+
+def assign_cells(chunk, at_axis):
+    return jnp.concatenate(
+        lax.all_to_all(
+            jnp.stack(tuple((chunk for _ in range(lax.axis_size(EXPERT)))), axis=0), EXPERT, 0, 0
+        ),
+        axis=at_axis,
+    )
+
+
+report_the_thing = functools.partial(assign_cells, at_axis=0)
 
 
 def shifted(value, axis, steps):
@@ -150,7 +163,7 @@
     counted = jnp.concatenate([doc_ids[1:], following[1]]) == doc_ids
     voc_start = lax.axis_index(EXPERT) * vocab_weight.shape[1]
     fresh = row_stats(
-        lax.all_gather(final_rows, EXPERT, axis=0, tiled=True),
+        report_the_thing(final_rows),
         lax.all_gather(targets, EXPERT, axis=0, tiled=True),
         vocab_weight,
         voc_start,

time: 300 us -> 507 us (1.69)
  waiting for transfers between devices: 67.7 us -> 211 us
  blocking collectives: 121 us -> 193 us
  between operations: 15 us -> 1.63 us
  local copies, waits for them, and re-layouts: 9.12 us -> 15.2 us
  starting transfers between devices: 8.66 us -> 13.9 us
    ppermute x2, waiting for transfers between devices: 0.01 us -> 183 us  [shifted(): lax.ppermute(value, axis, [(source, source + steps) for source in range(f...]
    all_gather x1, blocking collectives: 24.1 us -> 93.7 us  [local(): lax.all_gather(targets, EXPERT, axis=0, tiled=True)]
    all_gather x1 -> x0, waiting for transfers between devices: 39.9 us -> none  [local(): lax.all_gather(final_rows, EXPERT, axis=0, tiled=True)]
    another operation x1 -> x2, local copies, waits for them, and re-layouts: 0.01 us -> 6 us  [the longest x1 6 us: assign_cells(): jnp.stack(tuple((chunk for _ in range(lax.axis_size(EXPERT)))), axis=0)]
    all_to_all x0 -> x1, starting transfers between devices: none -> 5.73 us  [assign_cells(): lax.all_to_all(jnp.stack(tuple((chunk for _ in range(lax.axis_size(EXPERT...]
  transfers between devices with their start and end apart: 4 -> 4, of which waited for: 2 -> 2; matrix products, arithmetic and copies ran while one was open for 19% -> 10% of each run, Pallas kernels for 0% -> 0%
where the time goes in v1:
time: 507 us; the launch traced here: 506 us
  waiting for transfers between devices  211 us (42%)
  blocking collectives  193 us (38%)
  matrix products  51.8 us (10%)
  other arithmetic  19.4 us (4%)
  local copies, waits for them, and re-layouts  15.2 us (3%)
  starting transfers between devices  13.9 us (3%)
    ppermute x2, waiting for transfers between devices, shifted(): lax.ppermute(value, axis, [(source, source + steps) for source in range(f...  183 us
    all_gather x1, blocking collectives, local(): lax.all_gather(targets, EXPERT, axis=0, tiled=True)  93.7 us
    all_to_all x1, blocking collectives, local(): lax.all_to_all(outgoing, EXPERT, split_axis=0, concat_axis=0, tiled=True)  37.4 us
    psum x4, blocking collectives, by_axis(): value = lax.psum(value, axis)  32.7 us
    dot_general x8, matrix products, stats_block(): jnp.dot(hidden_rows, vocab_weight, preferred_element_type=jnp.float32)  32.5 us
    all_gather x3, blocking collectives, gathered_once(): both, at, found = (lax.all_gather(jnp.concatenate(lines), axis), 0, {})  29.2 us
    all_to_all x1, waiting for transfers between devices, local(): lax.all_to_all(expert_result, EXPERT, split_axis=0, concat_axis=0, tiled=...  27.9 us
    reduce_sum x8, other arithmetic, stats_block(): picked = jnp.sum(jnp.where(columns == wanted[:, None], scores, 0.0), axis=1)  11.3 us
  transfers between devices with their start and end apart: 4, of which 2 were waited for; matrix products, arithmetic and copies ran while one was open for 10% of the time, Pallas kernels for 0%

profile of v1, /device:TPU:1, one launch (start us, length us, event | category | flops | bytes accessed | tf_op | source)
XLA Modules:
  0.0 506.2 jit_solution(17490194737310076174)
XLA Ops:
  6.2 1.9 convolution_convert_fusion
  8.1 37.4 %all_to_all.15 = bf16[32,2,16,1024]{3,2,1,0:T(8,128)(2,1)S(1)} all-to-all(bf16[32,2,16,1024]{3,2,1,0:T(8,128)(2,1)S(1)} %bitcast.274), channel_id=1, replica_groups=mesh['dp'=4,'expert_0'=4,'expert_1'=4,'expert_2'=2] {'expert_0','expert_..., dimensions={0} | all-to-all | bytes 4194304 | tf_op jit(solution)/shard_map/all_to_all | solution.py:145
  45.5 4.3 fusion.8
  49.8 10.7 %convert_bitcast_fusion = bf16[32,2,16,1024]{3,2,0,1:T(8,128)(2,1)} fusion(bf16[2,1024,1024]{2,1,0:T(8,128)(2,1)} %param.18, f32[2,32,16,1024]{3,2,1,0:T(8,128)} %fusion.8, bf16[2,1024,1024]{2,1,0:T(8,128)(2,1)} %param.17, bf16[32,2,16,1024]{3,2,1,0:T(8,128)(2,1)S(1)} %all_to_all.15), kind=kOutput, calls=%fused_computation.21 | convolution fusion | flops 4302307328 | bytes 16777216 | tf_op jit(solution)/shard_map/sekf,efd->sekd/dot_general | solution.py:151
  60.5 3.3 copy.53
  63.8 4.0 all-to-all-start.1
  68.2 27.9 %all-to-all-done.1 = bf16[32,2,16,1024]{3,2,1,0:T(8,128)(2,1)S(1)} async-done(((bf16[32,2,16,1024]{3,2,1,0:T(8,128)(2,1)}), bf16[32,2,16,1024]{3,2,1,0:T(8,128)(2,1)S(1)}, u32[]{:S(2)}, u32[]{:S(2)}) %all-to-all-start.1) | async-done | bytes 2097184 | tf_op jit(solution)/shard_map/all_to_all | solution.py:154
  98.0 6.0 %stack.2 = bf16[32,256,1024]{2,1,0:T(8,128)(2,1)} broadcast(bf16[256,1024]{1,0:T(8,128)(2,1)S(1)} %multiply_convert_fusion), dimensions={1,2} | broadcast | bytes 17301504 | tf_op jit(solution)/shard_map/stack | solution.py:18
  104.0 5.7 %all-to-all-start.2 = ((bf16[32,256,1024]{2,1,0:T(8,128)(2,1)}), bf16[32,256,1024]{2,1,0:T(8,128)(2,1)}, u32[]{:S(2)}, u32[]{:S(2)}) async-start(bf16[32,256,1024]{2,1,0:T(8,128)(2,1)} %stack.2), calls=%async_computation.2 | async-start | bytes 33554432 | tf_op jit(solution)/shard_map/all_to_all | solution.py:17
  110.3 2.3 collective-permute-start.1
  113.2 1.9 collective-permute-start
  115.4 182.9 %collective-permute-done.1 = s32[1]{0:T(128)} collective-permute-done((s32[1]{0:T(128)}, s32[1]{0:T(128)}, u32[]{:S(2)}, u32[]{:S(2)}) %collective-permute-start.1) | collective-permute-done | bytes 36 | tf_op jit(solution)/shard_map/ppermute | solution.py:30
  299.0 93.7 %all-gather.3 = s32[32,1,256]{2,1,0:T(1,128)S(1)} all-gather(s32[1,1,256]{2,1,0:T(1,128)S(1)} %bitcast.293), channel_id=1, replica_groups=mesh['dp'=4,'expert_0'=4,'expert_1'=4,'expert_2'=2] {'expert_0','expert_..., dimensions={0}, use_global_device_ids=true | all-gather | bytes 33792 | tf_op jit(solution)/shard_map/all_gather | solution.py:167
  392.8 47.1 %while.14 = (s32[]{:T(128)}, f32[8,1024]{1,0:T(8,128)S(1)}, f32[8,1024]{1,0:T(8,128)S(1)}, f32[8,1024]{1,0:T(8,128)S(1)}, bf16[8,1024,1024]{2,1,0:T(8,128)(2,1)}...) while((s32[]{:T(128)}, f32[8,1024]{1,0:T(8,128)S(1)}, ...), condition=%wide.region_10.11_spmd, body=%wide.region_6.10_spmd.sunk | while | flops 2153773056 | bytes 12644985 | solution.py:85
  392.8 4.1 fusion.87
  398.7 4.1 fusion.87
  402.8 1.4 select_reduce_fusion.3
  404.6 4.1 fusion.87
  408.7 1.4 select_reduce_fusion.3
  410.5 4.1 fusion.87
  414.6 1.4 select_reduce_fusion.3
  416.4 4.1 fusion.87
  422.3 4.1 fusion.87
  428.1 4.1 fusion.87
  434.0 4.1 fusion.87
  440.1 12.8 %all-gather.4 = f32[4,3,8192]{2,1,0:T(4,128)S(1)} all-gather(f32[1,3,8192]{2,1,0:T(4,128)S(1)} %maximum_bitcast_fusion), channel_id=2, replica_groups=mesh['dp'=4,'expert_0'=4,'expert_1'=4,'expert_2'=2] {'expert_0'}, dimensions={0}, use_global_device_ids=true | all-gather | bytes 491520 | tf_op jit(solution)/shard_map/all_gather | solution.py:41
  453.5 10.4 %all-gather.5 = f32[4,3,8192]{2,1,0:T(4,128)S(1)} all-gather(f32[1,3,8192]{2,1,0:T(4,128)S(1)} %maximum_bitcast_fusion.1), channel_id=3, replica_groups=mesh['dp'=4,'expert_0'=4,'expert_1'=4,'expert_2'=2] {'expert_1'}, dimensions={0}, use_global_device_ids=true | all-gather | bytes 491520 | tf_op jit(solution)/shard_map/all_gather | solution.py:41
  464.5 5.9 %all-gather.6 = f32[2,3,8192]{2,1,0:T(4,128)S(1)} all-gather(f32[1,3,8192]{2,1,0:T(4,128)S(1)} %maximum_bitcast_fusion.2), channel_id=4, replica_groups=mesh['dp'=4,'expert_0'=4,'expert_1'=4,'expert_2'=2] {'expert_2'}, dimensions={0}, use_global_device_ids=true | all-gather | bytes 294912 | tf_op jit(solution)/shard_map/all_gather | solution.py:41
  471.6 8.7 %all-reduce.2 = (f32[512]{0:T(512)S(1)}, f32[512]{0:T(512)S(1)}) all-reduce(f32[512]{0:T(512)S(1)} %convert_reduce_fusion, f32[512]{0:T(512)S(1)} %bitcast.294), channel_id=1, replica_groups=mesh['dp'=4,'expert_0'=4,'expert_1'=4,'expert_2'=2] {'dp'}, use_global_device_ids=true, to_apply=%region_16.17 | all-reduce | flops 1024 | bytes 8192 | tf_op jit(solution)/shard_map/psum | solution.py:61
  480.4 9.1 %all-reduce.1 = (f32[512]{0:T(512)S(1)}, f32[512]{0:T(512)S(1)}) all-reduce(f32[512]{0:T(512)S(1)} %get-tuple-element.71, f32[512]{0:T(512)S(1)} %get-tuple-element.72), channel_id=1, replica_groups=mesh['dp'=4,'expert_0'=4,'expert_1'=4,'expert_2'=2] {'expert_0'}, use_global_device_ids=true, to_apply=%region_17.18 | all-reduce | flops 1024 | bytes 8192 | tf_op jit(solution)/shard_map/psum | solution.py:61
  489.5 6.3 %all-reduce = (f32[512]{0:T(512)S(1)}, f32[512]{0:T(512)S(1)}) all-reduce(f32[512]{0:T(512)S(1)} %get-tuple-element.69, f32[512]{0:T(512)S(1)} %get-tuple-element.70), channel_id=1, replica_groups=mesh['dp'=4,'expert_0'=4,'expert_1'=4,'expert_2'=2] {'expert_1'}, use_global_device_ids=true, to_apply=%region_18.19 | all-reduce | flops 1024 | bytes 8192 | tf_op jit(solution)/shard_map/psum | solution.py:61
  495.8 8.5 %all-reduce.3 = (f32[512]{0:T(512)S(1)}, f32[512]{0:T(512)S(1)}) all-reduce(f32[512]{0:T(512)S(1)} %get-tuple-element.67, f32[512]{0:T(512)S(1)} %get-tuple-element.68), channel_id=1, replica_groups=mesh['dp'=4,'expert_0'=4,'expert_1'=4,'expert_2'=2] {'expert_2'}, use_global_device_ids=true, to_apply=%region_19.20 | all-reduce | flops 1024 | bytes 8192 | tf_op jit(solution)/shard_map/psum | solution.py:61
  (120 shorter events, 23.5 us)
Async XLA Ops:
  0.6 67.1 %copy-start = (bf16[1024,64]{0,1:T(8,128)(2,1)S(1)}, bf16[1024,64]{0,1:T(8,128)(2,1)}, u32[]{:S(2)}) copy-start(bf16[1024,64]{0,1:T(8,128)(2,1)} %param.15) | copy-start | bytes 393220
  4.8 40.7 %copy-start.8 = (bf16[2,1024,1024]{2,1,0:T(8,128)(2,1)S(1)}, bf16[2,1024,1024]{2,1,0:T(8,128)(2,1)}, u32[]{:S(2)}) copy-start(bf16[2,1024,1024]{2,1,0:T(8,128)(2,1)} %param.16) | copy-start | bytes 12582916
  60.5 7.3 %copy-start.2 = (bf16[256,1024]{1,0:T(8,128)(2,1)S(1)}, bf16[256,1024]{1,0:T(8,128)(2,1)}, u32[]{:S(2)}) copy-start(bf16[256,1024]{1,0:T(8,128)(2,1)} %param.13) | copy-start | bytes 1572868
  60.5 7.3 %copy-start.10 = (f32[1024]{0:T(1024)S(1)}, f32[1024]{0:T(1024)}, u32[]{:S(2)}) copy-start(f32[1024]{0:T(1024)} %param.14) | copy-start | bytes 12292
  60.5 7.7 %copy-start.3 = (s32[256,2]{0,1:T(2,128)S(1)}, s32[256,2]{0,1:T(2,128)}, u32[]{:S(2)}) copy-start(s32[256,2]{0,1:T(2,128)} %param.23) | copy-start | bytes 6148
  63.8 32.3 %all-to-all-start.1 = ((bf16[32,2,16,1024]{3,2,1,0:T(8,128)(2,1)}), bf16[32,2,16,1024]{3,2,1,0:T(8,128)(2,1)S(1)}, u32[]{:S(2)}, u32[]{:S(2)}) async-start(bf16[32,2,16,1024]{3,2,1,0:T(8,128)(2,1)} %copy.53), calls=%async_computation.1 | async-start | bytes 4194304 | tf_op jit(solution)/shard_map/all_to_all | solution.py:154
  96.1 1.7 copy-start.5
  104.0 5.7 %copy-start.7 = (s32[256]{0:T(256)S(1)}, s32[256]{0:T(256)}, u32[]{:S(2)}) copy-start(s32[256]{0:T(256)} %param.21) | copy-start | bytes 3076
  104.0 8.7 %copy-start.4 = (s32[256]{0:T(256)S(1)}, s32[256]{0:T(256)}, u32[]{:S(2)}) copy-start(s32[256]{0:T(256)} %param.22) | copy-start | bytes 3076
  104.0 288.8 %copy-start.9 = (bf16[1024,1024]{1,0:T(8,128)(2,1)S(1)}, bf16[1024,1024]{1,0:T(8,128)(2,1)}, u32[]{:S(2)}) copy-start(bf16[1024,1024]{1,0:T(8,128)(2,1)} %param.20) | copy-start | bytes 6291460
  104.0 288.8 %all-to-all-start.2 = ((bf16[32,256,1024]{2,1,0:T(8,128)(2,1)}), bf16[32,256,1024]{2,1,0:T(8,128)(2,1)}, u32[]{:S(2)}, u32[]{:S(2)}) async-start(bf16[32,256,1024]{2,1,0:T(8,128)(2,1)} %stack.2), calls=%async_computation.2 | async-start | bytes 33554432 | tf_op jit(solution)/shard_map/all_to_all | solution.py:17
  110.3 188.0 %collective-permute-start.1 = (s32[1]{0:T(128)}, s32[1]{0:T(128)}, u32[]{:S(2)}, u32[]{:S(2)}) collective-permute-start(s32[1]{0:T(128)} %slice.204), channel_id=1, source_target_pairs={{1,0},{2,1},{3,2},{4,3},{5,4},{6,5},{7,6},{8,7},{9,8},{10,9},{11,1... | collective-permute-start | bytes 20 | tf_op jit(solution)/shard_map/ppermute | solution.py:30
  113.2 357.4 %collective-permute-start = (s32[1]{0:T(128)}, s32[1]{0:T(128)}, u32[]{:S(2)}, u32[]{:S(2)}) collective-permute-start(s32[1]{0:T(128)} %slice.194), channel_id=1, source_target_pairs={{1,0},{2,1},{3,2},{4,3},{5,4},{6,5},{7,6},{8,7},{9,8},{10,9},{11,1... | collective-permute-start | bytes 20 | tf_op jit(solution)/shard_map/ppermute | solution.py:30
  439.9 66.3 %copy-start.1 = (bf16[1024,64]{0,1:T(8,128)(2,1)S(1)}, bf16[1024,64]{0,1:T(8,128)(2,1)}, u32[]{:S(2)}) copy-start(bf16[1024,64]{0,1:T(8,128)(2,1)} %param.15) | copy-start | bytes 393220
  471.3 34.9 %copy-start.6 = (f32[256]{0:T(256)}, f32[256]{0:T(256)S(1)}, u32[]{:S(2)}) copy-start(f32[256]{0:T(256)S(1)} %compare_select_fusion) | copy-start | bytes 3076
